TPU v7x, 32 devices: a whole 2x2x4 slice. The times are simulated.
32 devices in a mesh: dp: 2 (over x), seq: 8 (over z, y), head: 2 (over core).
Axes of the slice: x: 2, y: 2, z: 4, core: 2. Of those that a mesh axis runs over, the one named last changes fastest.
Arguments:
- queries: bfloat16 [3072, 2048], P(('dp', 'seq'), 'head'), parts along dimension 0, may hold values from -6 to 6
- keys: bfloat16 [3072, 2048], P(('dp', 'seq'), 'head'), parts along dimension 0, may hold values from -6 to 6
- values: bfloat16 [3072, 2048], P(('dp', 'seq'), 'head'), parts along dimension 0, may hold values from -6 to 6
- segments: int32 [3072], P(('dp', 'seq')), parts along dimension 0, may hold values from 0 to 2, never falling along the last dimension, each value on 1 to 768 neighbouring positions
- hidden_in: bfloat16 [3072, 2048], P(('dp', 'seq', 'head')), parts along dimension 0, may hold values from -6 to 6
- attn_gain: float32 [2048], P('head'), may hold values from 0.25 to 1.75
- out_proj: bfloat16 [2048, 2048], P('head', 'seq'), may hold values from -0.125 to 0.125
- moe_gain: float32 [2048], replicated, may hold values from 0.1 to 1.9
- route_ids: int32 [3072, 8], P(('dp', 'seq', 'head')), parts along dimension 0, may hold values from 0 to 15, all different within a row; in each aligned block of 96 rows (0 to 95, 96 to 191, ...) at most 64 rows name the same one
- route_w: float32 [3072, 8], P(('dp', 'seq', 'head')), parts along dimension 0, may hold values from 0.02 to 0.5
- w_gate: bfloat16 [16, 2048, 768], P(('seq', 'head')), may hold values from -0.125 to 0.125
- w_up: bfloat16 [16, 2048, 768], P(('seq', 'head')), may hold values from -0.125 to 0.125
- w_down: bfloat16 [16, 768, 2048], P(('seq', 'head')), may hold values from -0.625 to 0.625
Outputs:
- block_out: bfloat16 [3072, 2048], P(('dp', 'seq', 'head')), parts along dimension 0
There are 2 independent parts, one for each index of `dp`. A program takes and returns all parts, laid end to end along the dimension named above; an argument that names none is the same for every part. Nothing has to cross between parts.
Inputs may be any that keep to these rules, and one draw needn't show every extreme that they name: `route_ids`: each row names 8 different experts. In the 96 rows of one device no expert is named more than 64 times; in some device's rows some expert is named exactly 64 times. `segments`: ids of 3 packed documents, never falling, every document at least one token, the longest exactly 768 tokens.
All inputs are finite; a program needn't handle non-finite values.
Results may differ from a plain program's by a relative error of at most 0.0065.
Values may be sent and summed in bfloat16 or wider, within the bound.
No kernel may reach another device: no remote copies, remote signals or barrier semaphores. Data moves between devices by JAX's collectives and lax.ppermute only.
A program may use at most 128 MiB of HBM per device.

v0:
```python
import jax
import jax.numpy as jnp
from jax import lax
from jax.sharding import PartitionSpec as P

D = 2048
DK = 128
TOPK = 8


epsilon = 1e-06


def carried_in(part, axis, combine, identity):
    place = lax.axis_index(axis)
    gathered = jax.tree.map(lambda a: lax.all_gather(a, axis), part)
    state = jax.tree.map(lambda a, e: jnp.zeros_like(a) + jnp.asarray(e, a.dtype), part, identity)

    def one(turn, state):
        return combine(
            state, jax.tree.map(lambda a: lax.dynamic_index_in_dim(a, turn, 0, False), gathered)
        )

    return lax.fori_loop(0, place, one, state)


def combine(earlier, later):
    first_one, last_one, state_one = earlier
    first_two, last_two, state_two = later
    keep_state = (first_two >= last_one) & (last_two <= last_one)
    merged = state_two + jnp.where(keep_state, state_one, jnp.zeros_like(state_one))
    return (jnp.minimum(first_one, first_two), jnp.maximum(last_one, last_two), merged)


def local(
    queries,
    keys,
    values,
    segments,
    hidden_in,
    attn_gain,
    out_proj,
    moe_gain,
    route_ids,
    route_w,
    w_gate,
    w_up,
    w_down,
):
    tok_rows = queries.shape[0]
    heads_here = attn_gain.shape[0] // DK
    query_rows = queries.reshape(tok_rows, heads_here, DK)
    key_rows = keys.reshape(tok_rows, heads_here, DK)
    value_rows = values.reshape(tok_rows, heads_here, DK)
    position = jnp.arange(tok_rows)
    causal = position[:, None] >= position[None, :]
    same_doc = (segments[:, None] == segments[None, :]) & causal
    scores = jnp.einsum("thd,shd->hts", query_rows, key_rows, preferred_element_type=jnp.float32)
    scores = jnp.where(same_doc[None], scores, 0.0)
    local_part = jnp.einsum(
        "hts,shd->thd", scores, value_rows.astype(jnp.float32), precision=lax.Precision.HIGHEST
    )
    tail_mask = (segments == segments[-1])[:, None, None]
    tail_keys = jnp.where(tail_mask, key_rows, jnp.zeros_like(key_rows))
    own_state = jnp.einsum(
        "thd,the->hde", tail_keys, value_rows, preferred_element_type=jnp.float32
    )
    first_seg = segments[0].astype(jnp.float32)
    last_seg = segments[-1].astype(jnp.float32)
    identity = (jnp.float32(1000000000.0), jnp.float32(-1.0), jnp.zeros_like(own_state))
    prefix_first, prefix_last, prefix_state = carried_in(
        (first_seg, last_seg, own_state), "seq", combine, identity
    )
    continued = (segments.astype(jnp.float32) == prefix_last)[:, None, None]
    carried_part = jnp.einsum(
        "thd,hde->the",
        query_rows.astype(jnp.float32),
        prefix_state,
        precision=lax.Precision.HIGHEST,
    )
    attn_raw = local_part + jnp.where(continued, carried_part, 0.0)
    mean_square = jnp.mean(attn_raw * attn_raw, axis=-1, keepdims=True)
    attended = attn_raw * lax.rsqrt(mean_square + epsilon) * attn_gain.reshape(heads_here, DK)
    attended = attended.astype(jnp.bfloat16).reshape(tok_rows, heads_here * DK)
    partial_out = jnp.dot(
        attended,
        lax.all_gather(out_proj, "seq", axis=1, tiled=True),
        preferred_element_type=jnp.float32,
    )
    attn_out = lax.psum_scatter(partial_out, "head", scatter_dimension=0, tiled=True)
    mid_wide = (hidden_in.astype(jnp.float32) + attn_out).astype(jnp.bfloat16).astype(jnp.float32)
    mid_square = jnp.mean(mid_wide * mid_wide, axis=-1, keepdims=True)
    normed = (mid_wide * lax.rsqrt(mid_square + epsilon) * moe_gain).astype(jnp.bfloat16)
    weights = route_w / jnp.sum(route_w, axis=1, keepdims=True)
    tok_dev = route_ids.shape[0]
    experts = lax.axis_size("seq") * lax.axis_size("head")
    capacity = 4 * tok_dev * TOPK // (3 * experts)
    flat_ids = route_ids.reshape(-1)
    labels = jnp.arange(experts, dtype=jnp.int32)
    onehot = (flat_ids[:, None] == labels[None, :]).astype(jnp.int32)
    before = jnp.cumsum(onehot, axis=0) - onehot
    slot_index = jnp.sum(before * onehot, axis=1)
    destination = (flat_ids * capacity + slot_index).reshape(tok_dev, TOPK)
    places = jnp.arange(experts * capacity, dtype=jnp.int32)
    selector = jnp.any(destination[None, :, :] == places[:, None, None], axis=2).astype(
        jnp.bfloat16
    )
    outgoing = jnp.dot(selector, normed, preferred_element_type=jnp.float32).astype(jnp.bfloat16)
    outgoing = outgoing.reshape(experts, capacity, D)
    arrived = lax.all_to_all(outgoing, ("seq", "head"), split_axis=0, concat_axis=0, tiled=True)
    row_shape = arrived.shape
    flat_rows = arrived.reshape(-1, row_shape[-1])
    gate_part = jnp.dot(flat_rows, w_gate[0], preferred_element_type=jnp.float32)
    up_part = jnp.dot(flat_rows, w_up[0], preferred_element_type=jnp.float32)
    inner = (jax.nn.silu(gate_part) * up_part).astype(jnp.bfloat16)
    answer = jnp.dot(inner, w_down[0], preferred_element_type=jnp.float32).astype(jnp.bfloat16)
    returned = lax.all_to_all(
        answer.reshape(row_shape), ("seq", "head"), split_axis=0, concat_axis=0, tiled=True
    )
    flat_out = returned.reshape(experts * capacity, D)
    picked = jnp.take(flat_out, destination.reshape(-1), axis=0).reshape(tok_dev, TOPK, D)
    mixture = jnp.sum(weights[:, :, None] * picked.astype(jnp.float32), axis=1)
    return (mid_wide + mixture).astype(jnp.bfloat16)


def solution(mesh):
    return jax.shard_map(
        local,
        mesh=mesh,
        in_specs=(
            P(("dp", "seq"), "head"),
            P(("dp", "seq"), "head"),
            P(("dp", "seq"), "head"),
            P(("dp", "seq")),
            P(("dp", "seq", "head"), None),
            P("head"),
            P("head", "seq"),
            P(),
            P(("dp", "seq", "head"), None),
            P(("dp", "seq", "head"), None),
            P(("seq", "head"), None, None),
            P(("seq", "head"), None, None),
            P(("seq", "head"), None, None),
        ),
        out_specs=P(("dp", "seq", "head"), None),
        check_vma=False,
    )
```

profile of v0, /device:TPU:13, one launch (start us, length us, event | category | flops | bytes accessed | tf_op | source)
XLA Modules:
  0.0 415.3 jit_solution(3173747557035355574)
XLA Ops:
  9.3 2.3 fusion.30
  16.5 13.0 %all-reduce.2 = (f32[8]{0:T(128)S(1)}, f32[8]{0:T(128)S(1)}) all-reduce(f32[8]{0:T(128)S(1)} %dynamic-update-slice, f32[8]{0:T(128)S(1)} %convert_dynamic-update-slice_fusion), channel_id=1, replica_groups=mesh['dp'=2,'seq'=8,'head'=2] {'seq'}, use_global_device_ids=true, to_apply=%add | all-reduce | flops 16 | bytes 128
  30.9 2.7 fusion.33
  33.7 49.3 %all-gather.6.cloned.1.call-done = f32[64,128,128]{2,1,0:T(8,128)} async-done(((f32[8,128,128]{2,1,0:T(8,128)}), f32[64,128,128]{2,1,0:T(8,128)}) %all-gather.6.cloned.1.call-update) | async-done | bytes 4194320 | tf_op jit(solution)/shard_map/all_gather | solution.py:16
  83.8 15.3 %while.14 = (s32[]{:T(128)}, f32[]{:T(128)}, f32[8,128,128]{2,1,0:T(8,128)}, s32[]{:T(128)}, f32[8]{0:T(128)S(1)}, /*index=5*/f32[8,8,128,128]{3,2,1,0:T(8,128)}, f32[8]{0:T(128)S(1)}, s32[]{:T(128)}, s32[]{:T(128)}, s32[]{:T(128)}) while((s32[]{:T(128)}, f32[]{:T(128)}, f32[8,128,128]{2,1,0:T(8,128)}, s32[]{:T(128)}, f32[8]{0:T(128)S(1)}, ...), condition=%wide.region_1.2_spmd, body=%wide.region_0.1_spmd.sunk | while | flops 262153 | bytes 1573061 | solution.py:24
  86.3 1.9 bitcast_add_fusion.2
  91.4 1.9 bitcast_add_fusion.2
  96.4 2.1 bitcast_add_fusion.2
  99.2 1.5 fusion.16
  100.7 3.3 multiply_reduce_fusion.1
  104.0 53.9 %all-gather.4.cloned.1.call-done = bf16[1024,2048]{1,0:T(8,128)(2,1)} async-done(((bf16[1024,256]{1,0:T(8,128)(2,1)}), bf16[1024,2048]{1,0:T(8,128)(2,1)}) %all-gather.4.cloned.1.call-update) | async-done | bytes 4194320 | tf_op jit(solution)/shard_map/all_gather | solution.py:87
  157.9 4.7 %fusion.27 = f32[192,2048]{1,0:T(8,128)} fusion(bf16[1024,2048]{1,0:T(8,128)(2,1)} %all-gather.4.cloned.1.call-done, f32[192,8,128]{2,0,1:T(8,128)} %get-tuple-element.87, f32[8,128]{1,0:T(8,128)S(1)} %bitcast.118, f32[192,8]{0,1:T(8,128)S(1)} %add_rsqrt_fusion), kind=kOutput, calls=%fused_computation.33 | convolution fusion | flops 805896192 | bytes 6563840 | tf_op jit(solution)/shard_map/dot_general | solution.py:85
  162.9 1.7 reduce-window.6
  165.8 1.7 fusion.5
  167.5 6.5 %reduce-scatter.2.cloned.1.call-done = f32[96,2048]{1,0:T(8,128)} async-done(((f32[192,2048]{1,0:T(8,128)}), f32[96,2048]{1,0:T(8,128)}) %reduce-scatter.2.cloned.1.call-update) | async-done | bytes 786448 | tf_op jit(solution)/shard_map/reduce_scatter | solution.py:90
  175.4 2.2 convolution_convert_fusion.1
  177.7 98.3 %all_to_all.10 = bf16[16,64,2048]{2,1,0:T(8,128)(2,1)S(1)} all-to-all(bf16[16,64,2048]{2,1,0:T(8,128)(2,1)S(1)} %bitcast.112), channel_id=1, replica_groups=mesh['dp'=2,'seq'=8,'head'=2] {'seq','head'}, dimensions={0} | all-to-all | bytes 8388608 | tf_op jit(solution)/shard_map/all_to_all | solution.py:110
  276.0 2.0 copy-done.1
  277.9 5.2 %fusion.1 = f32[1024,768]{1,0:T(8,128)} fusion(bf16[1024,2048]{1,0:T(8,128)(2,1)S(1)} %bitcast.114, bf16[1,2048,768]{2,1,0:T(8,128)(2,1)S(1)} %copy-done.6), kind=kOutput, calls=%fused_computation.7 | convolution fusion | flops 3221225472 | bytes 10485760 | tf_op jit(solution)/shard_map/dot_general | solution.py:114
  283.1 12.3 %convolution_convert_fusion = bf16[1024,2048]{1,0:T(8,128)(2,1)} fusion(bf16[1,768,2048]{2,1,0:T(8,128)(2,1)S(1)} %copy-done, f32[1024,768]{1,0:T(8,128)} %fusion.1, bf16[1024,2048]{1,0:T(8,128)(2,1)} %bitcast.115, bf16[1,2048,768]{2,1,0:T(8,128)(2,1)} %param.25), kind=kOutput, calls=%fused_computation.3 | convolution fusion | flops 6449266688 | bytes 17825792 | tf_op jit(solution)/shard_map/dot_general | solution.py:116
  295.4 5.2 %all-to-all-start.1 = ((bf16[16,64,2048]{2,1,0:T(8,128)(2,1)}), bf16[16,64,2048]{2,1,0:T(8,128)(2,1)}, u32[]{:S(2)}, u32[]{:S(2)}) async-start(bf16[16,64,2048]{2,1,0:T(8,128)(2,1)} %bitcast.113), calls=%async_computation.2 | async-start | bytes 8388608 | tf_op jit(solution)/shard_map/all_to_all | solution.py:117
  308.2 84.9 %all-to-all-done.1 = bf16[16,64,2048]{2,1,0:T(8,128)(2,1)} async-done(((bf16[16,64,2048]{2,1,0:T(8,128)(2,1)}), bf16[16,64,2048]{2,1,0:T(8,128)(2,1)}, u32[]{:S(2)}, u32[]{:S(2)}) %all-to-all-start.1) | async-done | bytes 4194336 | tf_op jit(solution)/shard_map/all_to_all | solution.py:117
  393.1 9.8 %gather_fusion = bf16[768,2048]{1,0:T(8,128)(2,1)} fusion(bf16[1024,2048]{1,0:T(8,128)(2,1)} %bitcast.17, s32[1024]{0:T(1024)S(1)} %pad_clamp_fusion), kind=kCustom, calls=%fused_computation | custom fusion | bytes 6294528 | tf_op jit(solution)/shard_map/jit(_take)/gather | solution.py:121
  402.9 5.0 %multiply_reduce_fusion = f32[96,2048]{1,0:T(8,128)S(1)} fusion(bf16[768,2048]{1,0:T(8,128)(2,1)} %gather_fusion, f32[96,8]{1,0:T(8,128)} %copy.62, pred[96,8]{1,0:T(8,128)(4,1)S(1)} %copy.67), kind=kLoop, calls=%fused_computation.2 | loop fusion | flops 6094848 | bytes 3936000 | tf_op jit(solution)/shard_map/reduce_sum | solution.py:122
  (59 shorter events, 24.3 us)
Async XLA Ops:
  6.5 276.6 %copy-start = (bf16[1,768,2048]{2,1,0:T(8,128)(2,1)S(1)}, bf16[1,768,2048]{2,1,0:T(8,128)(2,1)}, u32[]{:S(2)}) copy-start(bf16[1,768,2048]{2,1,0:T(8,128)(2,1)} %param.27) | copy-start | bytes 9437188
  6.5 76.5 %all-gather.6.cloned.1.call-start = ((), (), s32[]{:S(2)}) async-start(), calls=%async_computation.5 | async-start | bytes 4718592 | tf_op jit(solution)/shard_map/all_gather | solution.py:16
  11.6 146.3 %all-gather.4.cloned.1.call-start = ((), (), s32[]{:S(2)}) async-start(), calls=%async_computation.3 | async-start | bytes 4718592 | tf_op jit(solution)/shard_map/all_gather | solution.py:87
  12.4 161.6 %reduce-scatter.2.cloned.1.call-start = ((), (), s32[]{:S(2)}) async-start(), calls=%async_computation.4 | async-start | bytes 2359296 | tf_op jit(solution)/shard_map/reduce_scatter | solution.py:90
  83.8 15.3 %copy-start.4 = (s32[192]{0:T(256)S(1)}, s32[192]{0:T(256)}, u32[]{:S(2)}) copy-start(s32[192]{0:T(256)} %param.18) | copy-start | bytes 2308
  83.8 15.3 %copy-start.2 = (bf16[192,1024]{1,0:T(8,128)(2,1)S(1)}, bf16[192,1024]{1,0:T(8,128)(2,1)}, u32[]{:S(2)}) copy-start(bf16[192,1024]{1,0:T(8,128)(2,1)} %param.15) | copy-start | bytes 1179652
  99.1 58.8 %copy-start.5 = (f32[1024]{0:T(1024)S(1)}, f32[1024]{0:T(1024)}, u32[]{:S(2)}) copy-start(f32[1024]{0:T(1024)} %param.20) | copy-start | bytes 12292
  157.9 4.7 %copy-start.3 = (s32[96,8]{0,1:T(8,128)S(1)}, s32[96,8]{0,1:T(8,128)}, u32[]{:S(2)}) copy-start(s32[96,8]{0,1:T(8,128)} %param.23) | copy-start | bytes 9220
  177.7 100.3 %copy-start.6 = (bf16[1,2048,768]{2,1,0:T(8,128)(2,1)S(1)}, bf16[1,2048,768]{2,1,0:T(8,128)(2,1)}, u32[]{:S(2)}) copy-start(bf16[1,2048,768]{2,1,0:T(8,128)(2,1)} %param.26) | copy-start | bytes 9437188
  276.0 2.0 copy-start.1
  295.4 97.7 %all-to-all-start.1 = ((bf16[16,64,2048]{2,1,0:T(8,128)(2,1)}), bf16[16,64,2048]{2,1,0:T(8,128)(2,1)}, u32[]{:S(2)}, u32[]{:S(2)}) async-start(bf16[16,64,2048]{2,1,0:T(8,128)(2,1)} %bitcast.113), calls=%async_computation.2 | async-start | bytes 8388608 | tf_op jit(solution)/shard_map/all_to_all | solution.py:117
Sparse Core Ops, SparseCore 0:
  11.7 71.2 all-gather.5
  85.0 72.8 all-gather.3
  162.7 11.2 reduce-scatter.1
where the time goes:
time: 416 us; the launch traced here: 415 us
  waiting for transfers between devices  195 us (47%)
  blocking collectives  111 us (27%)
  matrix products  34.3 us (8%)
  local copies, waits for them, and re-layouts  24.8 us (6%)
  other arithmetic  24.7 us (6%)
  between operations  13.9 us (3%)
  loops' own time  5.69 us (1%)
  starting transfers between devices  5.3 us (1%)
    all_to_all x1, blocking collectives, local(): lax.all_to_all(outgoing, ('seq', 'head'), split_axis=0, concat_axis=0, ti...  98.3 us
    all_to_all x1, waiting for transfers between devices, local(): lax.all_to_all(answer.reshape(row_shape), ('seq', 'head'), split_axis=0,...  84.9 us
    all_gather x1, waiting for transfers between devices, local(): lax.all_gather(out_proj, 'seq', axis=1, tiled=True)  53.9 us
    all_gather x1, waiting for transfers between devices, carried_in(): gathered = jax.tree.map(lambda a: lax.all_gather(a, axis), part)  49.3 us
    unnamed x1, blocking collectives  13 us
    dot_general x1, matrix products, local(): jnp.dot(inner, w_down[0], preferred_element_type=jnp.float32)  12.3 us
    gather x1, local copies, waits for them, and re-layouts, local(): jnp.take(flat_out, destination.reshape(-1), axis=0)  9.83 us
  transfers between devices with their start and end apart: 4, of which 4 were waited for; matrix products, arithmetic and copies ran while one was open for 8% of the time, Pallas kernels for 0%

commit v1 on v0

v1 whole, which is shorter than its diff:
```python
import functools

import jax
import jax.numpy as jnp
from jax import lax
from jax.experimental import pallas as pl
from jax.experimental.pallas import tpu as pltpu
from jax.sharding import PartitionSpec as P


DK = 128
EPS = 1e-06
AUX = 16
BF = jnp.bfloat16
F32 = jnp.float32
FFN_VMEM = 24 << 20
SMALL_VMEM = 16 << 20


def dot(a, b):
    return jnp.dot(a, b, preferred_element_type=F32)


def ring_of(size):
    return list(range(0, size, 2)) + list(range(size - 1, 0, -2))


def hops(size):
    ring = ring_of(size)
    ahead = [(ring[i], ring[(i + 1) % size]) for i in range(size)]
    return ahead, [(b, a) for a, b in ahead]


def swap(x):
    return lax.ppermute(x, "head", [(0, 1), (1, 0)])


def ring_gather(x, axis):
    size = lax.axis_size("seq")
    ahead, back = hops(size)
    far = size // 2
    got = {0: x}
    up = down = x
    for k in range(1, far + 1):
        if k == far:
            mid = x.shape[axis] // 2
            up = lax.slice_in_dim(up, 0, mid, axis=axis)
            down = lax.slice_in_dim(down, mid, None, axis=axis)
        up = lax.ppermute(up, "seq", ahead)
        down = lax.ppermute(down, "seq", back)
        if k == far:
            got[far] = (up, down)
        else:
            got[-k], got[k] = up, down
    return got


def pieces(h, part):
    step = min(part, DK)
    for i in range(0, DK, step):
        yield (h * DK + i) // part, (h * DK + i) % part, i, step


def column(row, rows):
    return jnp.broadcast_to(row, (8, row.shape[1])).T[:rows, :1]


def state_kernel(seg_col, k_ref, v_ref, o_ref):
    part = o_ref.shape[1] - AUX
    rows = k_ref.shape[0]
    seg = seg_col[...]
    last = seg[rows - 1 :, :]
    tail = seg == last
    for h in range(k_ref.shape[1] // DK):
        cols = slice(h * DK, (h + 1) * DK)
        k = jnp.where(tail, k_ref[:, cols].astype(F32), 0.0).astype(BF)
        state = lax.dot_general(k, v_ref[:, cols], (((0,), (0,)), ((), ())), preferred_element_type=F32)
        for to, row, at, step in pieces(h, part):
            o_ref[to, row : row + step, :] = state[at : at + step, :].astype(BF)
    mark = jnp.broadcast_to(last.astype(F32), (AUX, DK)).astype(BF)
    for to in range(o_ref.shape[0]):
        o_ref[to, part:, :] = mark


def carry_kernel(me, c_ref, aux, o_ref, prev):
    part = o_ref.shape[1] - AUX
    size = o_ref.shape[0]
    carried = jnp.zeros((part, DK), F32)
    marks = [c_ref[s, part:, :].astype(F32)[:8] for s in range(size)]
    before = jnp.full((8, DK), -1.0, F32)
    for d in range(size):
        o_ref[d, :part, :] = carried.astype(BF)
        o_ref[d, part:, :] = aux[d]
        if d > 0:
            before = jnp.where(me[0] == d, marks[d - 1], before)
            going = marks[d - 1][:1] == marks[d][:1]
            carried = jnp.where(going, carried, 0.0)
        carried = carried + c_ref[d, :part, :].astype(F32)
    prev[...] = before


def attention_kernel(prev, seg_col, seg_row, q_ref, k_ref, v_ref, e_ref, g_ref, o_ref):
    rows = q_ref.shape[0]
    part = e_ref.shape[1] - AUX
    t = lax.broadcasted_iota(jnp.int32, (rows, rows), 0)
    s = lax.broadcasted_iota(jnp.int32, (rows, rows), 1)
    seg = seg_col[...]
    same = (seg == seg_row[...]) & (t >= s)
    continued = seg.astype(F32) == prev[:1, :]
    for h in range(q_ref.shape[1] // DK):
        cols = slice(h * DK, (h + 1) * DK)
        q, v = q_ref[:, cols], v_ref[:, cols]
        score = lax.dot_general(q, k_ref[:, cols], (((1,), (1,)), ((), ())), preferred_element_type=F32)
        score = jnp.where(same, score, 0.0)
        high = score.astype(BF)
        low = (score - high.astype(F32)).astype(BF)
        entering = jnp.concatenate([e_ref[to, row : row + step, :] for to, row, _, step in pieces(h, part)], axis=0)
        raw = dot(high, v) + dot(low, v) + jnp.where(continued, dot(q, entering), 0.0)
        square = jnp.mean(raw * raw, axis=1, keepdims=True)
        o_ref[:, cols] = (raw * lax.rsqrt(square + EPS) * g_ref[:, cols]).astype(BF)


def projection_kernel(order, att, *rest):
    w_refs, keep, give = rest[:-2], rest[-2], rest[-1]
    tok = keep.shape[0]
    core = order[len(w_refs) - 1]
    width, half = w_refs[0].shape[1], att.shape[1] // 2
    x = att[...]

    def put(i, y):
        at = pl.ds(pl.multiple_of(order[i] * width, width), width)
        a, b = y[:tok], y[tok:]
        keep[:, at] = jnp.where(core == 0, a, b)
        give[:, at] = jnp.where(core == 0, b, a)

    for i, w in enumerate(w_refs[:-2]):
        put(i, dot(x, w[...]))
    put(len(w_refs) - 2, dot(x[:, :half], w_refs[-2][...]) + dot(x[:, half:], w_refs[-1][...]))


def ffn_kernel(rows, parts, which, owner, own, other, *rest):
    n = len(parts)
    x_refs, (wg, wu, wd), o_refs = rest[:n], rest[n : n + 3], rest[n + 3 : 2 * n + 3]
    xs, inner = rest[2 * n + 3 :]
    for (unit, col), x in zip(parts, x_refs):
        xs[unit * rows : (unit + 1) * rows, col : col + x.shape[1]] = x[...]
    ff, d = wd.shape[1:]
    block = 256 if ff % 256 == 0 else ff

    def hidden(j, _):
        at = pl.ds(pl.multiple_of(j * block, block), block)
        gate, up = dot(xs[...], wg[0, :, at]), dot(xs[...], wu[0, :, at])
        inner[:, at] = (gate / (1.0 + jnp.exp(-gate)) * up).astype(BF)
        return 0

    lax.fori_loop(0, ff // block, hidden, 0)
    scale = [column((own, other)[u % 2][pl.ds(owner[which[u // 2]], 1), :], rows) for u in range(2 * len(which))]
    width = 512
    o_cols = o_refs[0].shape[1]

    for start in range(0, d, o_cols):
        mine = [(unit, o) for (unit, col), o in zip(parts, o_refs) if col == start]

        def result(j, _):
            y = dot(inner[...], wd[0, :, pl.ds(pl.multiple_of(start + j * width, width), width)]).astype(BF).astype(F32)
            for unit, o in mine:
                o[:, pl.ds(pl.multiple_of(j * width, width), width)] = (y[unit * rows : (unit + 1) * rows] * scale[unit]).astype(BF)
            return 0

        lax.fori_loop(0, o_cols // width, result, 0)


VMEM = pl.BlockSpec(memory_space=pltpu.VMEM)
SMEM = pl.BlockSpec(memory_space=pltpu.SMEM)


def expert(parts, which, owner, xs, own, other, w_gate, w_up, w_down):
    rows = xs[0].shape[0]
    d, ff = w_gate.shape[1:]
    total = 2 * len(which) * rows
    return pl.pallas_call(
        functools.partial(ffn_kernel, rows, parts, which),
        in_specs=[SMEM] + [VMEM] * (5 + len(xs)),
        out_specs=[VMEM] * len(xs),
        out_shape=[jax.ShapeDtypeStruct(x.shape, BF) for x in xs],
        scratch_shapes=[pltpu.VMEM((total, d), BF), pltpu.VMEM((total, ff), BF)],
        compiler_params=pltpu.CompilerParams(vmem_limit_bytes=FFN_VMEM),
        cost_estimate=pl.CostEstimate(flops=6 * total * d * ff, bytes_accessed=4 * total * d, transcendentals=total * ff),
    )(owner, own, other, *xs, w_gate, w_up, w_down)


def local(queries, keys, values, segments, hidden_in, attn_gain, out_proj, moe_gain, route_ids, route_w, w_gate, w_up, w_down):
    size, cores = lax.axis_size("seq"), lax.axis_size("head")
    me, core = lax.axis_index("seq"), lax.axis_index("head")
    ring = ring_of(size)
    far = size // 2
    place = jnp.asarray([ring.index(i) for i in range(size)], jnp.int32)[me]
    offsets = [0] + [r for k in range(1, far) for r in (-k, k)] + [far]
    owners = jnp.asarray(ring, jnp.int32)[(place + jnp.asarray(offsets, jnp.int32)) % size]
    rows, heads = queries.shape[0], queries.shape[1] // DK
    tok, d = hidden_in.shape
    small = pltpu.CompilerParams(vmem_limit_bytes=SMALL_VMEM)

    w_got = ring_gather(out_proj, 0)
    w_parts = [w_got[r] for r in offsets[:-1]] + list(w_got[far])

    seg_col, seg_row = segments[:, None], segments[None, :]
    part = heads * DK // size
    block = jax.ShapeDtypeStruct((size, part + AUX, DK), BF)
    sent = pl.pallas_call(state_kernel, out_shape=block, compiler_params=small)(seg_col, keys, values)
    came = lax.all_to_all(sent, "seq", split_axis=0, concat_axis=0, tiled=True)

    weights = route_w / jnp.sum(route_w, axis=1, keepdims=True)
    experts = jnp.arange(size * cores, dtype=jnp.int32)
    dense = jnp.sum(jnp.where(route_ids.T[None] == experts[:, None, None], weights.T[None], 0.0), axis=1)
    dense = jnp.pad(dense, ((0, 0), (0, DK - tok))).reshape(size, cores, DK)
    high = dense.astype(BF)
    low = (dense - high.astype(F32)).astype(BF)
    aux = jnp.concatenate([high, low, jnp.zeros((size, AUX - 2 * cores, DK), BF)], axis=1)
    carried, prev = pl.pallas_call(
        carry_kernel,
        in_specs=[SMEM, VMEM, VMEM],
        out_specs=[VMEM, VMEM],
        out_shape=[block, jax.ShapeDtypeStruct((8, DK), F32)],
        compiler_params=small,
    )(me[None], came, aux)
    entering = lax.all_to_all(carried, "seq", split_axis=0, concat_axis=0, tiled=True)
    att = pl.pallas_call(
        attention_kernel, out_shape=jax.ShapeDtypeStruct((rows, heads * DK), BF), compiler_params=small
    )(prev, seg_col, seg_row, queries, keys, values, entering, attn_gain[None, :])

    scale = entering[:, part : part + cores].astype(F32) + entering[:, part + cores : part + 2 * cores].astype(F32)
    own = lax.dynamic_index_in_dim(scale, core, 1, False)
    other = swap(lax.dynamic_index_in_dim(scale, 1 - core, 1, False))

    if out_proj.shape[1] % 128:
        full = jnp.stack([w_got[r] for r in offsets[:-1]] + [jnp.concatenate(w_got[far], axis=0)])
        full = full[jnp.argsort(owners)].transpose(1, 0, 2).reshape(heads * DK, d)
        mid_row = heads * DK // 2
        w_parts, order = [full[:mid_row], full[mid_row:]], jnp.stack([jnp.int32(0), core])
    else:
        order = jnp.concatenate([owners, core[None]])
    keep, give = pl.pallas_call(
        projection_kernel,
        in_specs=[SMEM] + [VMEM] * (1 + len(w_parts)),
        out_specs=[VMEM, VMEM],
        out_shape=[jax.ShapeDtypeStruct((tok, d), F32)] * 2,
        compiler_params=small,
    )(order, att, *w_parts)
    give = swap(give)
    mid = (hidden_in.astype(F32) + (keep + give)).astype(BF).astype(F32)
    square = jnp.mean(mid * mid, axis=-1, keepdims=True)
    normed = (mid * lax.rsqrt(square + EPS) * moe_gain).astype(BF)

    x_got = ring_gather(normed, 1)
    cut = d // 2
    out = {}
    for k in range(far + 1):
        group = [0] if k == 0 else [far] if k == far else [-k, k]
        parts, xs = [], []
        for r in group:
            for i, x in enumerate(x_got[r] if r == far else (x_got[r],)):
                y = swap(x)
                parts += [(2 * group.index(r), i * cut), (2 * group.index(r) + 1, i * cut)]
                xs += [x, y]
        which = tuple(offsets.index(r) for r in group)
        ys = expert(tuple(parts), which, owners, xs, own, other, w_gate, w_up, w_down)
        i = 0
        for r in group:
            both = []
            for _ in range(2 if r == far else 1):
                both.append((ys[i], swap(ys[i + 1])))
                i += 2
            out[r] = both if r == far else both[0]

    ahead, back = hops(size)
    add = lambda *a: sum(x.astype(F32) for x in a)
    up = lax.ppermute(add(*out[far][0]).astype(BF), "seq", ahead)
    down = lax.ppermute(add(*out[far][1]).astype(BF), "seq", back)
    for k in range(far - 1, 0, -1):
        u, v = add(*out[k]), add(*out[-k])
        if k == far - 1:
            u = jnp.concatenate([u[:, :cut] + up.astype(F32), u[:, cut:]], axis=1)
            v = jnp.concatenate([v[:, :cut], v[:, cut:] + down.astype(F32)], axis=1)
        else:
            u, v = u + up.astype(F32), v + down.astype(F32)
        up = lax.ppermute(u.astype(BF), "seq", ahead)
        down = lax.ppermute(v.astype(BF), "seq", back)
    return (mid + (add(*out[0]) + add(up, down))).astype(BF)


def solution(mesh):
    rows = P(("dp", "seq", "head"), None)
    packed = P(("dp", "seq"), "head")
    expert_spec = P(("seq", "head"), None, None)
    return jax.shard_map(
        local,
        mesh=mesh,
        in_specs=(
            packed, packed, packed, P(("dp", "seq")), rows, P("head"), P("head", "seq"), P(), rows, rows,
            expert_spec, expert_spec, expert_spec,
        ),
        out_specs=rows,
        check_vma=False,
    )
```

time: 416 us -> 196 us (0.47)
  the two profiles are of different devices: /device:TPU:13 before, /device:TPU:0 now
where the time goes in v1:
time: 196 us; the launch traced here: 195 us
  waiting for transfers between devices  86.8 us (44%)
  starting transfers between devices  47.3 us (24%)
  Pallas kernels  31.4 us (16%)
  local copies, waits for them, and re-layouts  21.5 us (11%)
  other arithmetic  7.98 us (4%)
    ppermute x8, waiting for transfers between devices, ring_gather(): up = lax.ppermute(up, 'seq', ahead)  36.7 us
    pallas_call x5, Pallas kernels, expert(): pl.pallas_call(functools.partial(ffn_kernel, rows, parts, which), in_spec...  26.1 us
    ppermute x8, starting transfers between devices, ring_gather(): up = lax.ppermute(up, 'seq', ahead)  21.8 us
    ppermute x3, waiting for transfers between devices, local(): down = lax.ppermute(v.astype(BF), 'seq', back)  19.8 us
    unnamed x64, local copies, waits for them, and re-layouts  16.3 us
    ppermute x3, waiting for transfers between devices, local(): up = lax.ppermute(u.astype(BF), 'seq', ahead)  8.12 us
    all_to_all x1, starting transfers between devices, local(): came = lax.all_to_all(sent, 'seq', split_axis=0, concat_axis=0, tiled=True)  6.06 us
    ppermute x20, waiting for transfers between devices, swap(): return lax.ppermute(x, 'head', [(0, 1), (1, 0)])  5.92 us
  transfers between devices with their start and end apart: 46, of which 16 were waited for; matrix products, arithmetic and copies ran while one was open for 6% of the time, Pallas kernels for 15%

profile of v1, /device:TPU:0, one launch (start us, length us, event | category | flops | bytes accessed | tf_op | source)
XLA Modules:
  0.0 195.4 jit_solution(6038355061364236979)
XLA Ops:
  0.0 3.1 %collective-permute-start = (bf16[1024,256]{1,0:T(8,128)(2,1)}, bf16[1024,256]{1,0:T(8,128)(2,1)S(1)}, u32[]{:S(2)}, u32[]{:S(2)}) collective-permute-start(bf16[1024,256]{1,0:T(8,128)(2,1)} %rest_0_.1), channel_id=1, source_target_pairs={{0,4},{4,8},{8,12},{12,14},{14,10},{10,6},{6,2},{2,0},{1,5},{5,9},... | collective-permute-start | bytes 1572872 | tf_op jit(solution)/shard_map/ppermute | solution.py:49
  3.1 12.1 %collective-permute-done.rest_1_ = bf16[1024,256]{1,0:T(8,128)(2,1)S(1)} collective-permute-done((bf16[1024,256]{1,0:T(8,128)(2,1)}, bf16[1024,256]{1,0:T(8,128)(2,1)S(1)}, u32[]{:S(2)}, u32[]{:S(2)}) %collective-permute-start) | collective-permute-done | bytes 524320 | tf_op jit(solution)/shard_map/ppermute | solution.py:49
  21.1 6.1 %all-to-all-start = ((bf16[8,144,128]{2,1,0:T(8,128)(2,1)}), bf16[8,144,128]{2,1,0:T(8,128)(2,1)S(1)}, u32[]{:S(2)}, u32[]{:S(2)}) async-start(bf16[8,144,128]{2,1,0:T(8,128)(2,1)} %shard_map.154), calls=%async_computation | async-start | bytes 589824 | tf_op jit(solution)/shard_map/all_to_all | solution.py:211
  28.6 3.0 %collective-permute-start.4 = (bf16[1024,256]{1,0:T(8,128)(2,1)S(1)}, bf16[1024,256]{1,0:T(8,128)(2,1)S(1)}, u32[]{:S(2)}, u32[]{:S(2)}) collective-permute-start(bf16[1024,256]{1,0:T(8,128)(2,1)S(1)} %collective-permute-done.2.rest_3_), channel_id=1, source_target_pairs={{0,4},{4,8},{8,12},{12,14},{14,10},{10,6},{6,2},{2,0},{1,5},{5,9},... | collective-permute-start | bytes 1572872 | tf_op jit(solution)/shard_map/ppermute | solution.py:49
  32.7 5.6 %all-to-all-done.c_ref = bf16[8,144,128]{2,1,0:T(8,128)(2,1)S(1)} async-done(((bf16[8,144,128]{2,1,0:T(8,128)(2,1)}), bf16[8,144,128]{2,1,0:T(8,128)(2,1)S(1)}, u32[]{:S(2)}, u32[]{:S(2)}) %all-to-all-start) | async-done | bytes 294944 | tf_op jit(solution)/shard_map/all_to_all | solution.py:211
  39.1 3.5 %all-to-all-start.1 = ((bf16[8,144,128]{2,1,0:T(8,128)(2,1)}), bf16[8,144,128]{2,1,0:T(8,128)(2,1)S(1)}, u32[]{:S(2)}, u32[]{:S(2)}) async-start(bf16[8,144,128]{2,1,0:T(8,128)(2,1)} %copy-done.24), calls=%async_computation.1 | async-start | bytes 589824 | tf_op jit(solution)/shard_map/all_to_all | solution.py:227
  45.3 5.9 %collective-permute-start.6 = (bf16[512,256]{1,0:T(8,128)(2,1)}, bf16[512,256]{1,0:T(8,128)(2,1)S(1)}, u32[]{:S(2)}, u32[]{:S(2)}) collective-permute-start(bf16[512,256]{1,0:T(8,128)(2,1)} %slice.44), channel_id=1, source_target_pairs={{0,4},{4,8},{8,12},{12,14},{14,10},{10,6},{6,2},{2,0},{1,5},{5,9},... | collective-permute-start | bytes 786440 | tf_op jit(solution)/shard_map/ppermute | solution.py:49
  70.0 2.3 %collective-permute-done.8 = f32[96,2048]{1,0:T(8,128)S(1)} collective-permute-done((f32[96,2048]{1,0:T(8,128)S(1)}, f32[96,2048]{1,0:T(8,128)S(1)}, u32[]{:S(2)}, u32[]{:S(2)}) %collective-permute-start.8) | collective-permute-done | bytes 786464 | tf_op jit(solution)/shard_map/ppermute | solution.py:35
  72.7 2.9 %collective-permute-start.12 = (bf16[96,2048]{1,0:T(8,128)(2,1)S(1)}, bf16[96,2048]{1,0:T(8,128)(2,1)}, u32[]{:S(2)}, u32[]{:S(2)}) collective-permute-start(bf16[96,2048]{1,0:T(8,128)(2,1)S(1)} %fusion.2.rest_0_), channel_id=1, source_target_pairs={{0,4},{4,8},{8,12},{12,14},{14,10},{10,6},{6,2},{2,0},{1,5},{5,9},... | collective-permute-start | bytes 1179656 | tf_op jit(solution)/shard_map/ppermute | solution.py:49
  75.6 9.0 %collective-permute-done.12.rest_0_ = bf16[96,2048]{1,0:T(8,128)(2,1)} collective-permute-done((bf16[96,2048]{1,0:T(8,128)(2,1)S(1)}, bf16[96,2048]{1,0:T(8,128)(2,1)}, u32[]{:S(2)}, u32[]{:S(2)}) %collective-permute-start.12) | collective-permute-done | bytes 393248 | tf_op jit(solution)/shard_map/ppermute | solution.py:49
  84.6 2.2 %collective-permute-start.17 = (bf16[96,2048]{1,0:T(8,128)(2,1)}, bf16[96,2048]{1,0:T(8,128)(2,1)}, u32[]{:S(2)}, u32[]{:S(2)}) collective-permute-start(bf16[96,2048]{1,0:T(8,128)(2,1)} %collective-permute-done.12.rest_0_), channel_id=1, source_target_pairs={{0,4},{4,8},{8,12},{12,14},{14,10},{10,6},{6,2},{2,0},{1,5},{5,9},... | collective-permute-start | bytes 1179656 | tf_op jit(solution)/shard_map/ppermute | solution.py:49
  86.9 8.9 %collective-permute-done.17.rest_0_ = bf16[96,2048]{1,0:T(8,128)(2,1)} collective-permute-done((bf16[96,2048]{1,0:T(8,128)(2,1)}, bf16[96,2048]{1,0:T(8,128)(2,1)}, u32[]{:S(2)}, u32[]{:S(2)}) %collective-permute-start.17) | collective-permute-done | bytes 393248 | tf_op jit(solution)/shard_map/ppermute | solution.py:49
  100.0 6.0 %collective-permute-done.22.rest_0_ = bf16[96,2048]{1,0:T(8,128)(2,1)S(1)} collective-permute-done((bf16[96,2048]{1,0:T(8,128)(2,1)}, bf16[96,2048]{1,0:T(8,128)(2,1)S(1)}, u32[]{:S(2)}, u32[]{:S(2)}) %collective-permute-start.22) | collective-permute-done | bytes 393248 | tf_op jit(solution)/shard_map/ppermute | solution.py:49
  109.8 3.9 %shard_map.158 = (bf16[96,2048]{1,0:T(8,128)(2,1)S(1)}, bf16[96,2048]{1,0:T(8,128)(2,1)S(1)}) custom-call(s32[8]{0:T(128)S(1)} %gather_fusion, f32[8,128]{1,0:T(8,128)S(1)} %bitcast.12, f32[8,128]{1,0:T(8,128)S(1)} %collective-permute-done.9.other, bf16[96,2048]{1,0:T(8,128)(2,1)S(1)} %fusion.2.rest_0_, ...), custom_call_target="tpu_custom_call" | custom-call | flops 1811939328 | bytes 1572864 | tf_op jit(solution)/shard_map/pallas_call | solution.py:181
  116.4 6.3 %shard_map.159 = (bf16[96,2048]{1,0:T(8,128)(2,1)S(1)}, bf16[96,2048]{1,0:T(8,128)(2,1)S(1)}, bf16[96,2048]{1,0:T(8,128)(2,1)S(1)}, bf16[96,2048]{1,0:T(8,128)(2,1)S(1)}) custom-call(s32[8]{0:T(128)S(1)} %gather_fusion, f32[8,128]{1,0:T(8,128)S(1)} %bitcast.13, f32[8,128]{1,0:T(8,128)S(1)} %collective-permute-done.9.other, ...), custom_call_target="tpu_custom_call" | custom-call | flops 3623878656 | bytes 3145728 | tf_op jit(solution)/shard_map/pallas_call | solution.py:181
  123.8 6.3 %shard_map.160 = (bf16[96,2048]{1,0:T(8,128)(2,1)S(1)}, bf16[96,2048]{1,0:T(8,128)(2,1)S(1)}, bf16[96,2048]{1,0:T(8,128)(2,1)S(1)}, bf16[96,2048]{1,0:T(8,128)(2,1)S(1)}) custom-call(s32[8]{0:T(128)S(1)} %gather_fusion, f32[8,128]{1,0:T(8,128)S(1)} %bitcast.14, f32[8,128]{1,0:T(8,128)S(1)} %collective-permute-done.9.other, ...), custom_call_target="tpu_custom_call" | custom-call | flops 3623878656 | bytes 3145728 | tf_op jit(solution)/shard_map/pallas_call | solution.py:181
  130.7 3.9 %shard_map.162 = (bf16[96,1024]{1,0:T(8,128)(2,1)S(1)}, bf16[96,1024]{1,0:T(8,128)(2,1)S(1)}, bf16[96,1024]{1,0:T(8,128)(2,1)S(1)}, bf16[96,1024]{1,0:T(8,128)(2,1)S(1)}) custom-call(s32[8]{0:T(128)S(1)} %gather_fusion, f32[8,128]{1,0:T(8,128)S(1)} %bitcast.15, f32[8,128]{1,0:T(8,128)S(1)} %collective-permute-done.9.other, ...), custom_call_target="tpu_custom_call" | custom-call | flops 1811939328 | bytes 1572864 | tf_op jit(solution)/shard_map/pallas_call | solution.py:181
  134.8 5.7 %shard_map.161 = (bf16[96,2048]{1,0:T(8,128)(2,1)S(1)}, bf16[96,2048]{1,0:T(8,128)(2,1)S(1)}, bf16[96,2048]{1,0:T(8,128)(2,1)S(1)}, bf16[96,2048]{1,0:T(8,128)(2,1)S(1)}) custom-call(s32[8]{0:T(128)S(1)} %gather_fusion, f32[8,128]{1,0:T(8,128)S(1)} %bitcast.16, f32[8,128]{1,0:T(8,128)S(1)} %collective-permute-done.9.other, ...), custom_call_target="tpu_custom_call" | custom-call | flops 3623878656 | bytes 3145728 | tf_op jit(solution)/shard_map/pallas_call | solution.py:181
  146.3 5.9 %collective-permute-done.32 = bf16[96,1024]{1,0:T(8,128)(2,1)S(1)} collective-permute-done((bf16[96,1024]{1,0:T(8,128)(2,1)S(1)}, bf16[96,1024]{1,0:T(8,128)(2,1)S(1)}, u32[]{:S(2)}, u32[]{:S(2)}) %collective-permute-start.32) | collective-permute-done | bytes 196640 | tf_op jit(solution)/shard_map/ppermute | solution.py:278
  153.7 4.8 %collective-permute-done.40 = bf16[96,1024]{1,0:T(8,128)(2,1)S(1)} collective-permute-done((bf16[96,1024]{1,0:T(8,128)(2,1)S(1)}, bf16[96,1024]{1,0:T(8,128)(2,1)S(1)}, u32[]{:S(2)}, u32[]{:S(2)}) %collective-permute-start.40) | collective-permute-done | bytes 196640 | tf_op jit(solution)/shard_map/ppermute | solution.py:279
  160.0 8.1 %collective-permute-done.33 = bf16[96,2048]{1,0:T(8,128)(2,1)S(1)} collective-permute-done((bf16[96,2048]{1,0:T(8,128)(2,1)S(1)}, bf16[96,2048]{1,0:T(8,128)(2,1)S(1)}, u32[]{:S(2)}, u32[]{:S(2)}) %collective-permute-start.33) | collective-permute-done | bytes 393248 | tf_op jit(solution)/shard_map/ppermute | solution.py:287
  170.4 6.7 %collective-permute-done.41 = bf16[96,2048]{1,0:T(8,128)(2,1)S(1)} collective-permute-done((bf16[96,2048]{1,0:T(8,128)(2,1)S(1)}, bf16[96,2048]{1,0:T(8,128)(2,1)S(1)}, u32[]{:S(2)}, u32[]{:S(2)}) %collective-permute-start.41) | collective-permute-done | bytes 393248 | tf_op jit(solution)/shard_map/ppermute | solution.py:288
  179.6 6.8 %collective-permute-done.42 = bf16[96,2048]{1,0:T(8,128)(2,1)S(1)} collective-permute-done((bf16[96,2048]{1,0:T(8,128)(2,1)S(1)}, bf16[96,2048]{1,0:T(8,128)(2,1)S(1)}, u32[]{:S(2)}, u32[]{:S(2)}) %collective-permute-start.42) | collective-permute-done | bytes 393248 | tf_op jit(solution)/shard_map/ppermute | solution.py:288
  188.2 6.2 %collective-permute-done.43 = bf16[96,2048]{1,0:T(8,128)(2,1)S(1)} collective-permute-done((bf16[96,2048]{1,0:T(8,128)(2,1)S(1)}, bf16[96,2048]{1,0:T(8,128)(2,1)S(1)}, u32[]{:S(2)}, u32[]{:S(2)}) %collective-permute-start.43) | collective-permute-done | bytes 393248 | tf_op jit(solution)/shard_map/ppermute | solution.py:288
  (179 shorter events, 59.7 us)
Async XLA Ops:
  0.0 15.1 %collective-permute-start = (bf16[1024,256]{1,0:T(8,128)(2,1)}, bf16[1024,256]{1,0:T(8,128)(2,1)S(1)}, u32[]{:S(2)}, u32[]{:S(2)}) collective-permute-start(bf16[1024,256]{1,0:T(8,128)(2,1)} %rest_0_.1), channel_id=1, source_target_pairs={{0,4},{4,8},{8,12},{12,14},{14,10},{10,6},{6,2},{2,0},{1,5},{5,9},... | collective-permute-start | bytes 1572872 | tf_op jit(solution)/shard_map/ppermute | solution.py:49
  3.1 13.9 %collective-permute-start.1 = (bf16[1024,256]{1,0:T(8,128)(2,1)}, bf16[1024,256]{1,0:T(8,128)(2,1)S(1)}, u32[]{:S(2)}, u32[]{:S(2)}) collective-permute-start(bf16[1024,256]{1,0:T(8,128)(2,1)} %rest_0_.1), channel_id=1, source_target_pairs={{4,0},{8,4},{12,8},{14,12},{10,14},{6,10},{2,6},{0,2},{5,1},{9,5},... | collective-permute-start | bytes 1572872 | tf_op jit(solution)/shard_map/ppermute | solution.py:50
  15.1 13.5 %collective-permute-start.2 = (bf16[1024,256]{1,0:T(8,128)(2,1)S(1)}, bf16[1024,256]{1,0:T(8,128)(2,1)S(1)}, u32[]{:S(2)}, u32[]{:S(2)}) collective-permute-start(bf16[1024,256]{1,0:T(8,128)(2,1)S(1)} %collective-permute-done.rest_1_), channel_id=1, source_target_pairs={{0,4},{4,8},{8,12},{12,14},{14,10},{10,6},{6,2},{2,0},{1,5},{5,9},... | collective-permute-start | bytes 1572872 | tf_op jit(solution)/shard_map/ppermute | solution.py:49
  16.9 14.7 %collective-permute-start.3 = (bf16[1024,256]{1,0:T(8,128)(2,1)S(1)}, bf16[1024,256]{1,0:T(8,128)(2,1)S(1)}, u32[]{:S(2)}, u32[]{:S(2)}) collective-permute-start(bf16[1024,256]{1,0:T(8,128)(2,1)S(1)} %collective-permute-done.1.rest_2_), channel_id=1, source_target_pairs={{4,0},{8,4},{12,8},{14,12},{10,14},{6,10},{2,6},{0,2},{5,1},{9,5},... | collective-permute-start | bytes 1572872 | tf_op jit(solution)/shard_map/ppermute | solution.py:50
  21.1 17.2 %all-to-all-start = ((bf16[8,144,128]{2,1,0:T(8,128)(2,1)}), bf16[8,144,128]{2,1,0:T(8,128)(2,1)S(1)}, u32[]{:S(2)}, u32[]{:S(2)}) async-start(bf16[8,144,128]{2,1,0:T(8,128)(2,1)} %shard_map.154), calls=%async_computation | async-start | bytes 589824 | tf_op jit(solution)/shard_map/all_to_all | solution.py:211
  28.6 16.0 %collective-permute-start.4 = (bf16[1024,256]{1,0:T(8,128)(2,1)S(1)}, bf16[1024,256]{1,0:T(8,128)(2,1)S(1)}, u32[]{:S(2)}, u32[]{:S(2)}) collective-permute-start(bf16[1024,256]{1,0:T(8,128)(2,1)S(1)} %collective-permute-done.2.rest_3_), channel_id=1, source_target_pairs={{0,4},{4,8},{8,12},{12,14},{14,10},{10,6},{6,2},{2,0},{1,5},{5,9},... | collective-permute-start | bytes 1572872 | tf_op jit(solution)/shard_map/ppermute | solution.py:49
  31.7 19.6 %collective-permute-start.5 = (bf16[1024,256]{1,0:T(8,128)(2,1)S(1)}, bf16[1024,256]{1,0:T(8,128)(2,1)S(1)}, u32[]{:S(2)}, u32[]{:S(2)}) collective-permute-start(bf16[1024,256]{1,0:T(8,128)(2,1)S(1)} %collective-permute-done.3.rest_4_), channel_id=1, source_target_pairs={{4,0},{8,4},{12,8},{14,12},{10,14},{6,10},{2,6},{0,2},{5,1},{9,5},... | collective-permute-start | bytes 1572872 | tf_op jit(solution)/shard_map/ppermute | solution.py:50
  39.1 16.9 %all-to-all-start.1 = ((bf16[8,144,128]{2,1,0:T(8,128)(2,1)}), bf16[8,144,128]{2,1,0:T(8,128)(2,1)S(1)}, u32[]{:S(2)}, u32[]{:S(2)}) async-start(bf16[8,144,128]{2,1,0:T(8,128)(2,1)} %copy-done.24), calls=%async_computation.1 | async-start | bytes 589824 | tf_op jit(solution)/shard_map/all_to_all | solution.py:227
  45.3 14.5 %collective-permute-start.6 = (bf16[512,256]{1,0:T(8,128)(2,1)}, bf16[512,256]{1,0:T(8,128)(2,1)S(1)}, u32[]{:S(2)}, u32[]{:S(2)}) collective-permute-start(bf16[512,256]{1,0:T(8,128)(2,1)} %slice.44), channel_id=1, source_target_pairs={{0,4},{4,8},{8,12},{12,14},{14,10},{10,6},{6,2},{2,0},{1,5},{5,9},... | collective-permute-start | bytes 786440 | tf_op jit(solution)/shard_map/ppermute | solution.py:49
  72.7 11.9 %collective-permute-start.12 = (bf16[96,2048]{1,0:T(8,128)(2,1)S(1)}, bf16[96,2048]{1,0:T(8,128)(2,1)}, u32[]{:S(2)}, u32[]{:S(2)}) collective-permute-start(bf16[96,2048]{1,0:T(8,128)(2,1)S(1)} %fusion.2.rest_0_), channel_id=1, source_target_pairs={{0,4},{4,8},{8,12},{12,14},{14,10},{10,6},{6,2},{2,0},{1,5},{5,9},... | collective-permute-start | bytes 1179656 | tf_op jit(solution)/shard_map/ppermute | solution.py:49
  75.6 11.3 %collective-permute-start.14 = (bf16[96,2048]{1,0:T(8,128)(2,1)S(1)}, bf16[96,2048]{1,0:T(8,128)(2,1)}, u32[]{:S(2)}, u32[]{:S(2)}) collective-permute-start(bf16[96,2048]{1,0:T(8,128)(2,1)S(1)} %fusion.2.rest_0_), channel_id=1, source_target_pairs={{4,0},{8,4},{12,8},{14,12},{10,14},{6,10},{2,6},{0,2},{5,1},{9,5},... | collective-permute-start | bytes 1179656 | tf_op jit(solution)/shard_map/ppermute | solution.py:50
  86.8 11.5 %collective-permute-start.19 = (bf16[96,2048]{1,0:T(8,128)(2,1)}, bf16[96,2048]{1,0:T(8,128)(2,1)}, u32[]{:S(2)}, u32[]{:S(2)}) collective-permute-start(bf16[96,2048]{1,0:T(8,128)(2,1)} %collective-permute-done.14.rest_2_), channel_id=1, source_target_pairs={{4,0},{8,4},{12,8},{14,12},{10,14},{6,10},{2,6},{0,2},{5,1},{9,5},... | collective-permute-start | bytes 1179656 | tf_op jit(solution)/shard_map/ppermute | solution.py:50
  86.8 12.8 %collective-permute-start.10 = (bf16[96,2048]{1,0:T(8,128)(2,1)S(1)}, bf16[96,2048]{1,0:T(8,128)(2,1)S(1)}, u32[]{:S(2)}, u32[]{:S(2)}) collective-permute-start(bf16[96,2048]{1,0:T(8,128)(2,1)S(1)} %fusion.2.rest_0_), channel_id=1, source_target_pairs={{0,1},{1,0},{2,3},{3,2},{4,5},{5,4},{6,7},{7,6},{8,9},{9,8},{10,11... | collective-permute-start | bytes 1179656 | tf_op jit(solution)/shard_map/ppermute | solution.py:35
  98.4 15.4 %collective-permute-start.24 = (bf16[96,2048]{1,0:T(8,128)(2,1)}, bf16[96,2048]{1,0:T(8,128)(2,1)S(1)}, u32[]{:S(2)}, u32[]{:S(2)}) collective-permute-start(bf16[96,2048]{1,0:T(8,128)(2,1)} %collective-permute-done.19.rest_2_), channel_id=1, source_target_pairs={{4,0},{8,4},{12,8},{14,12},{10,14},{6,10},{2,6},{0,2},{5,1},{9,5},... | collective-permute-start | bytes 1179656 | tf_op jit(solution)/shard_map/ppermute | solution.py:50
  98.8 15.5 %collective-permute-start.13 = (bf16[96,2048]{1,0:T(8,128)(2,1)}, bf16[96,2048]{1,0:T(8,128)(2,1)S(1)}, u32[]{:S(2)}, u32[]{:S(2)}) collective-permute-start(bf16[96,2048]{1,0:T(8,128)(2,1)} %collective-permute-done.12.rest_0_), channel_id=1, source_target_pairs={{0,1},{1,0},{2,3},{3,2},{4,5},{5,4},{6,7},{7,6},{8,9},{9,8},{10,11... | collective-permute-start | bytes 1179656 | tf_op jit(solution)/shard_map/ppermute | solution.py:35
  99.5 16.0 %collective-permute-start.15 = (bf16[96,2048]{1,0:T(8,128)(2,1)}, bf16[96,2048]{1,0:T(8,128)(2,1)S(1)}, u32[]{:S(2)}, u32[]{:S(2)}) collective-permute-start(bf16[96,2048]{1,0:T(8,128)(2,1)} %collective-permute-done.14.rest_2_), channel_id=1, source_target_pairs={{0,1},{1,0},{2,3},{3,2},{4,5},{5,4},{6,7},{7,6},{8,9},{9,8},{10,11... | collective-permute-start | bytes 1179656 | tf_op jit(solution)/shard_map/ppermute | solution.py:35
  99.7 23.0 %collective-permute-start.18 = (bf16[96,2048]{1,0:T(8,128)(2,1)}, bf16[96,2048]{1,0:T(8,128)(2,1)S(1)}, u32[]{:S(2)}, u32[]{:S(2)}) collective-permute-start(bf16[96,2048]{1,0:T(8,128)(2,1)} %collective-permute-done.17.rest_0_), channel_id=1, source_target_pairs={{0,1},{1,0},{2,3},{3,2},{4,5},{5,4},{6,7},{7,6},{8,9},{9,8},{10,11... | collective-permute-start | bytes 1179656 | tf_op jit(solution)/shard_map/ppermute | solution.py:35
  106.0 16.8 %collective-permute-start.20 = (bf16[96,2048]{1,0:T(8,128)(2,1)}, bf16[96,2048]{1,0:T(8,128)(2,1)S(1)}, u32[]{:S(2)}, u32[]{:S(2)}) collective-permute-start(bf16[96,2048]{1,0:T(8,128)(2,1)} %collective-permute-done.19.rest_2_), channel_id=1, source_target_pairs={{0,1},{1,0},{2,3},{3,2},{4,5},{5,4},{6,7},{7,6},{8,9},{9,8},{10,11... | collective-permute-start | bytes 1179656 | tf_op jit(solution)/shard_map/ppermute | solution.py:35
  113.7 74.4 %collective-permute-start.11 = (bf16[96,2048]{1,0:T(8,128)(2,1)S(1)}, bf16[96,2048]{1,0:T(8,128)(2,1)S(1)}, u32[]{:S(2)}, u32[]{:S(2)}) collective-permute-start(bf16[96,2048]{1,0:T(8,128)(2,1)S(1)} %get-tuple-element.32), channel_id=1, source_target_pairs={{0,1},{1,0},{2,3},{3,2},{4,5},{5,4},{6,7},{7,6},{8,9},{9,8},{10,11... | collective-permute-start | bytes 1179656 | tf_op jit(solution)/shard_map/ppermute | solution.py:35
  122.7 11.9 %collective-permute-start.23 = (bf16[96,2048]{1,0:T(8,128)(2,1)S(1)}, bf16[96,2048]{1,0:T(8,128)(2,1)S(1)}, u32[]{:S(2)}, u32[]{:S(2)}) collective-permute-start(bf16[96,2048]{1,0:T(8,128)(2,1)S(1)} %collective-permute-done.22.rest_0_), channel_id=1, source_target_pairs={{0,1},{1,0},{2,3},{3,2},{4,5},{5,4},{6,7},{7,6},{8,9},{9,8},{10,11... | collective-permute-start | bytes 1179656 | tf_op jit(solution)/shard_map/ppermute | solution.py:35
  122.8 12.0 %collective-permute-start.25 = (bf16[96,2048]{1,0:T(8,128)(2,1)S(1)}, bf16[96,2048]{1,0:T(8,128)(2,1)S(1)}, u32[]{:S(2)}, u32[]{:S(2)}) collective-permute-start(bf16[96,2048]{1,0:T(8,128)(2,1)S(1)} %collective-permute-done.24.rest_2_), channel_id=1, source_target_pairs={{0,1},{1,0},{2,3},{3,2},{4,5},{5,4},{6,7},{7,6},{8,9},{9,8},{10,11... | collective-permute-start | bytes 1179656 | tf_op jit(solution)/shard_map/ppermute | solution.py:35
  130.2 48.7 %collective-permute-start.16 = (bf16[96,2048]{1,0:T(8,128)(2,1)S(1)}, bf16[96,2048]{1,0:T(8,128)(2,1)S(1)}, u32[]{:S(2)}, u32[]{:S(2)}) collective-permute-start(bf16[96,2048]{1,0:T(8,128)(2,1)S(1)} %get-tuple-element.34), channel_id=1, source_target_pairs={{0,1},{1,0},{2,3},{3,2},{4,5},{5,4},{6,7},{7,6},{8,9},{9,8},{10,11... | collective-permute-start | bytes 1179656 | tf_op jit(solution)/shard_map/ppermute | solution.py:35
  130.3 49.2 %collective-permute-start.36 = (bf16[96,2048]{1,0:T(8,128)(2,1)S(1)}, bf16[96,2048]{1,0:T(8,128)(2,1)S(1)}, u32[]{:S(2)}, u32[]{:S(2)}) collective-permute-start(bf16[96,2048]{1,0:T(8,128)(2,1)S(1)} %get-tuple-element.42), channel_id=1, source_target_pairs={{0,1},{1,0},{2,3},{3,2},{4,5},{5,4},{6,7},{7,6},{8,9},{9,8},{10,11... | collective-permute-start | bytes 1179656 | tf_op jit(solution)/shard_map/ppermute | solution.py:35
  142.7 17.3 %collective-permute-start.21 = (bf16[96,2048]{1,0:T(8,128)(2,1)S(1)}, bf16[96,2048]{1,0:T(8,128)(2,1)S(1)}, u32[]{:S(2)}, u32[]{:S(2)}) collective-permute-start(bf16[96,2048]{1,0:T(8,128)(2,1)S(1)} %get-tuple-element.36), channel_id=1, source_target_pairs={{0,1},{1,0},{2,3},{3,2},{4,5},{5,4},{6,7},{7,6},{8,9},{9,8},{10,11... | collective-permute-start | bytes 1179656 | tf_op jit(solution)/shard_map/ppermute | solution.py:35
  (54 other events, 577.9 us)
